TPU v7x, 32 devices: a whole 2x2x4 slice. The times are simulated.
32 devices in a mesh: comp: 2 (over y), lat: 4 (over x, core), lon: 4 (over z).
Axes of the slice: x: 2, y: 2, z: 4, core: 2. Of those that a mesh axis runs over, the one named last changes fastest.
Arguments:
- state: float32 [2, 3, 32, 64, 512], P('comp', None, None, 'lat', 'lon'), may hold values from -6 to 6
- wave_push: float32 [2, 32], P('comp'), may hold values from 0.2 to 0.6
- wave_fill: float32 [2, 32], P('comp'), may hold values from 0.2 to 0.6
- vertical: float32 [2, 32, 32], P('comp'), may hold values from -0.5 to 1
- land_mask: int32 [64, 512], P('lat', 'lon'), may hold values 0 or 1
- tile_match: int32 [4, 4, 2], P('lat'), may hold values from 0 to 3, as said below
- cell_counts: int32 [4, 4, 2], P('lat'), may hold values from 16 to 2032, as said below
Outputs:
- advanced: float32 [2, 3, 32, 64, 512], P('comp', None, None, 'lat', 'lon')
Inputs may be any that keep to these rules, and one draw needn't show every extreme that they name: tile_match(i, j, 0) = j, and tile_match(i, j, 1) is j - 1 or j + 1 taken modulo 4. cell_counts(i, j, 0) + cell_counts(i, j, 1) = 2048, with both entries positive multiples of 16.
All inputs are finite; a program needn't handle non-finite values. No bound on the sum of `land_mask` on one device may be relied on, other than what follows from the above.
Results may differ from a plain program's by a relative error of at most 0.0001.
Values sent between devices are 32-bit elements; how exact they have to be, the bound alone decides.
A program may use at most 64 MiB of HBM per device.

v0:
```python
import functools
import math

import jax
import jax.numpy as jnp
from jax import lax
from jax.experimental import pallas as pl
from jax.experimental.pallas import tpu as pltpu
from jax.sharding import PartitionSpec as P

KAPPA = 0.5
CORIOLIS = 0.4
MESH = pl.DeviceIdType.MESH
HALO = 4
SPAN = 8
SETS = 3
ORDER = (1, 0, 2)
SLOTS = (0, 1, 4, 5)
U, V, PR = 0, 1, 2


class Layout:
    def __init__(self, rows, cols):
        self.blocks = cols // SPAN
        self.half = self.blocks // 2
        own = range(HALO, rows + HALO)
        assert rows * SPAN == cols and rows + 2 * HALO <= SETS * self.half
        self.dense, self.shift, self.span = {}, {}, {}
        at = 0
        for r in ORDER:
            mine = [e for e in own if e % SETS == r]
            self.shift[r] = mine[0] // SETS - at
            self.span[r] = (mine[0] // SETS, mine[-1] // SETS)
            for e in mine:
                self.dense[e - HALO] = at
                at += 1
        self.beyond = ((HALO - 2, HALO - 1), (rows + HALO, rows + HALO + 1))
        self.north = self.beyond[1][0] // SETS - self.beyond[0][0] // SETS
        for k in (0, 1):
            low, high = self.beyond[0][k], self.beyond[1][k]
            assert low % SETS == high % SETS and low // SETS == k
            assert high // SETS == self.north + k
        taken = [
            (s + self.corner(side, ns)) % self.blocks
            for side in (0, 1)
            for ns in (0, 1)
            for s in SLOTS
        ]
        assert len(set(taken)) == len(taken)

    def corner(self, side, ns):
        return self.half * side + self.north * ns


def exchange(
    sizes,
    state,
    push_in,
    fill_in,
    vert_in,
    land_in,
    match_in,
    count_in,
    main,
    edge,
    flux,
    ext,
    mid,
    vone,
    vtwo,
    part,
    dense,
    push_v,
    fill_v,
    vert_v,
    land_v,
    match_v,
    count_v,
    own_s,
    land_y,
    side_out,
    side_in,
    corner_out,
    corner_in,
    surf,
    load_sem,
    send_sem,
    recv_sem,
):
    levels, rows, cols, n_lat, n_lon = sizes
    plan = Layout(rows, cols)
    groups = levels // 8
    comp = lax.axis_index("comp")
    lat = lax.axis_index("lat")
    lon = lax.axis_index("lon")
    west = lax.rem(lon + n_lon - 1, n_lon)
    east = lax.rem(lon + 1, n_lon)
    other = 1 - comp
    has = (lat > 0, lat < n_lat - 1)
    beside = (lat - 1, lat + 1)

    barrier = pltpu.get_barrier_semaphore()

    def greet(to):
        pl.semaphore_signal(barrier, inc=1, device_id=to, device_id_type=MESH)

    greet((comp, lat, west))
    greet((comp, lat, east))
    greet((other, lat, lon))
    for ns in (0, 1):

        @pl.when(has[ns])
        def _(ns=ns):
            for there in (west, east, lon):
                greet((comp, beside[ns], there))

    small = (
        (push_in, push_v),
        (fill_in, fill_v),
        (vert_in, vert_v),
        (land_in, land_v),
        (match_in, match_v),
        (count_in, count_v),
        (state.at[:, 0], own_s),
    )
    first = HALO
    last = HALO + rows - 1
    for f in (PR, U, V):
        for y in range(rows):
            pltpu.make_async_copy(
                state.at[f, :, y, :], ext.at[f, first + y], load_sem.at[f]
            ).start()
    loads = [
        pltpu.make_async_copy(src, dst, load_sem.at[3 + k])
        for k, (src, dst) in enumerate(small)
    ]
    for copy in loads:
        copy.start()

    def wait_field(f):
        own = ext.at[f, pl.ds(first, rows)]
        pltpu.make_async_copy(own, own, load_sem.at[f]).wait()

    for ns in (0, 1):

        @pl.when(jnp.logical_not(has[ns]))
        def _(ns=ns):
            start = 0 if ns == 0 else first + rows
            for f in (U, V, PR):
                ext[f, pl.ds(start, HALO)] = jnp.zeros((HALO, levels, cols), jnp.float32)
            land_y[ns] = jnp.zeros((8, cols), jnp.int32)
            for side in (0, 1):
                corner_in[side, ns] = jnp.zeros((8, cols), jnp.float32)

    @pl.when(has[0])
    def _():
        ext[U, 0] = jnp.zeros((levels, cols), jnp.float32)
        ext[V, 0] = jnp.zeros((levels, cols), jnp.float32)

    @pl.when(has[1])
    def _():
        ext[U, last + HALO] = jnp.zeros((levels, cols), jnp.float32)
        ext[V, last + HALO] = jnp.zeros((levels, cols), jnp.float32)

    present = [flag.astype(jnp.float32) for flag in has]
    lane = lax.broadcasted_iota(jnp.int32, (levels, cols), 1)
    lane8 = lax.broadcasted_iota(jnp.int32, (8, cols), 1)
    j, block = lax.rem(lane, SPAN), lane // SPAN
    j8, block8 = lax.rem(lane8, SPAN), lane8 // SPAN
    west8 = block8 < plan.half
    by_size = {levels: (j, block), 8: (j8, block8)}

    def is_own(size):
        jj, blk = by_size[size]
        return ((blk < plan.half) & (jj >= HALO)) | ((blk >= plan.half) & (jj < HALO))

    stack = lambda x: jnp.concatenate([x] * groups, axis=0)

    def coriolis(row):
        angle = (row.astype(jnp.float32) + 0.5) / (n_lat * rows) - 0.5
        return CORIOLIS * jnp.sin(math.pi * angle)

    base_row = lat * rows - HALO
    fcor = coriolis(
        lax.broadcasted_iota(jnp.int32, (rows + 2 * HALO, cols), 0) + base_row
    )
    local8 = lax.rem(block8, plan.half)
    strip_fcor = [stack(coriolis(SETS * local8 + r + base_row)) for r in range(SETS)]

    def roll(x, by):
        by = by % cols
        return pltpu.roll(x, by, 1) if by else x

    def pack(row):
        result = None
        for y in range(rows):
            d = plan.dense[y]
            turned = roll(row(y), SPAN * d + HALO)
            where = (block if turned.shape[0] == levels else block8) == d
            result = turned if result is None else jnp.where(where, turned, result)
        return result

    def pack_field(f):
        wait_field(f)
        packed = pack(lambda y: ext[f, first + y])
        dense[f] = packed
        return packed

    low = j < HALO
    qp = pack_field(PR)
    qu = pack_field(U)
    side_out[0, pl.ds(0, levels)] = jnp.where(low, qp, roll(qu, HALO))
    side_out[1, pl.ds(0, levels)] = jnp.where(low, roll(qu, -HALO), qp)
    qv = pack_field(V)
    mid_level = levels // 2
    half_low = low[:mid_level]
    v_low, v_high = qv[:mid_level], qv[mid_level:]
    side_out[0, pl.ds(levels, mid_level)] = jnp.where(half_low, v_low, roll(v_high, HALO))
    side_out[1, pl.ds(levels, mid_level)] = jnp.where(half_low, roll(v_high, -HALO), v_low)
    for copy in loads[:4]:
        copy.wait()
    dry = comp == 1
    mask = jnp.where(dry, land_v[...].astype(jnp.float32), 1.0)
    spread = jnp.broadcast_to
    qm = pack(lambda y: spread(mask[y : y + 1], (8, cols)))
    side_out[0, pl.ds(levels + mid_level, 8)] = qm
    side_out[1, pl.ds(levels + mid_level, 8)] = qm

    turn = {PR: 0, U: -2, V: 2}
    for ns in (0, 1):
        its = 1 - ns
        picked = (0, 1) if ns == 0 else (rows - 2, rows - 1)
        found = {}
        for f in (U, V, PR):
            total = jnp.zeros((8, cols), jnp.float32)
            for k, y in enumerate(picked):
                value = ext[f, first + y]
                for g in range(groups):
                    b = (SLOTS[g] + plan.corner(0, its) + 2 * k) % plan.blocks
                    piece = roll(value[8 * g : 8 * g + 8], SPAN * b + HALO + turn[f])
                    total = jnp.where(block8 == b, piece, total)
            found[f] = total
        to_east = jnp.where(j8 < 2, found[U], jnp.where(j8 < 4, found[PR], found[V]))
        to_west = jnp.where(j8 < 4, found[U], jnp.where(j8 < 6, found[PR], found[V]))
        corner_out[ns, 0] = to_east
        corner_out[ns, 1] = roll(to_west, SPAN * plan.half)

    def remote(src, dst, sent, got, to):
        return pltpu.make_async_remote_copy(
            src_ref=src,
            dst_ref=dst,
            send_sem=send_sem.at[sent],
            recv_sem=recv_sem.at[got],
            device_id=to,
            device_id_type=MESH,
        )

    def side_copy(k, to):
        return remote(side_out.at[k], side_in.at[k], k, k, (comp, lat, to))

    sides = [side_copy(0, east), side_copy(1, west)]

    def corner_copies(ns):
        return [
            remote(
                corner_out.at[ns, side],
                corner_in.at[side, 1 - ns],
                2 + 2 * ns + side,
                2 + 2 * (1 - ns) + side,
                (comp, beside[ns], (east, west)[side]),
            )
            for side in (0, 1)
        ]

    def row_copies(ns):
        its = 1 - ns
        base, peer = 6 + 3 * ns, 6 + 3 * its
        to = (comp, beside[ns], lon)
        if ns == 0:
            p_from, p_to, w_from, w_to = first, first + rows, first, first + rows
        else:
            p_from, p_to, w_from, w_to = last + 1 - HALO, 0, last + 2 - HALO, 1
        return [
            remote(
                ext.at[PR, pl.ds(p_from, HALO)],
                ext.at[PR, pl.ds(p_to, HALO)],
                base,
                peer,
                to,
            ),
            remote(
                ext.at[pl.ds(0, 2), pl.ds(w_from, HALO - 1)],
                ext.at[pl.ds(0, 2), pl.ds(w_to, HALO - 1)],
                base + 1,
                peer + 1,
                to,
            ),
            remote(
                land_in.at[pl.ds(0 if ns == 0 else rows - 8, 8)],
                land_y.at[its],
                base + 2,
                peer + 2,
                to,
            ),
        ]

    across = remote(state.at[:, 0], surf.at[0], 12, 12, (other, lat, lon))
    onward = [
        remote(surf.at[0], surf.at[k], 12 + k, 12 + k, (comp, lat, to))
        for k, to in ((1, east), (2, west))
    ]

    count_there = [flag.astype(jnp.int32) for flag in has]
    pl.semaphore_wait(barrier, 3 + 3 * (count_there[0] + count_there[1]))
    for copy in reversed(sides):
        copy.start()
    for ns in (0, 1):

        @pl.when(has[ns])
        def _(ns=ns):
            for copy in corner_copies(ns) + row_copies(ns):
                copy.start()

    across.start()

    diag = lax.broadcasted_iota(jnp.int32, (levels, levels), 0) == lax.broadcasted_iota(
        jnp.int32, (levels, levels), 1
    )

    def per_level(ref):
        wide = spread(ref[...], (levels, levels))
        column = jnp.sum(jnp.where(diag, wide, 0.0), axis=1, keepdims=True)
        return spread(column * 0.5, (levels, cols))

    hp = per_level(push_v)
    hf = per_level(fill_v)
    vert = vert_v[...]
    vert_hi = vert.astype(jnp.bfloat16).astype(jnp.float32)
    vert_cat = jnp.concatenate([vert_hi, vert_hi, vert - vert_hi], axis=1).astype(
        jnp.bfloat16
    )

    def split(x):
        hi = x.astype(jnp.bfloat16)
        lo = (x - hi.astype(jnp.float32)).astype(jnp.bfloat16)
        return jnp.concatenate([hi, lo, hi], axis=0)

    def product(pieces):
        result = jnp.dot(
            vert_cat,
            jnp.concatenate([split(x) for x in pieces], axis=1),
            preferred_element_type=jnp.float32,
        )
        return [result[:, i * cols : (i + 1) * cols] for i in range(len(pieces))]

    is_first, is_last = lane == 0, lane == cols - 1

    def span_x(x):
        return jnp.where(is_last, 0.0, roll(x, -1)) - jnp.where(is_first, 0.0, roll(x, 1))

    beyond_mask = []

    def keep(e):
        if e < first:
            return beyond_mask[0][e + 8 - first : e + 9 - first]
        if e > last:
            return beyond_mask[1][e - last - 1 : e - last]
        return mask[e - first : e - first + 1]

    def force(e):
        return fcor[e : e + 1]

    def advance_v(read, store, es):
        for e in es:
            v1 = read(V, e) - hp * (read(PR, e + 1) - read(PR, e - 1)) - force(e) * read(U, e)
            if e == first - 1:
                v1 = present[0] * v1
            if e == last + 1:
                v1 = present[1] * v1
            store[e] = v1

    def advance_u(read, e):
        u1 = read(U, e) + force(e) * read(V, e) - hp * span_x(read(PR, e))
        return u1, read(PR, e) - hf * span_x(u1)

    def add_v(store, e, value):
        return value - hf * (store[e + 1] - store[e - 1])

    def read_one(f, e):
        return ext[f, e]

    def read_two(f, e):
        return mid[f, e]

    def write_mid(f, e, value):
        mid[f, e] = keep(e) * value

    def write_main(f, e, value):
        main[f, e - first] = keep(e) * value

    def run(read, store, write, v_rows, u_rows, p_rows, v_kept, slot):
        advance_v(read, store, v_rows)
        for e in v_kept:
            write(V, e, store[e])
        ready = {}
        for e in u_rows:
            u1, partial = advance_u(read, e)
            write(U, e, u1)
            if e in p_rows:
                ready[e] = add_v(store, e, partial)
            else:
                part[slot[e]] = partial
        for e in p_rows:
            if e not in ready:
                ready[e] = add_v(store, e, part[slot[e]])
        for e, value in zip(p_rows, product([ready[e] for e in p_rows])):
            write(PR, e, value)

    slot_one = {first: 0, first + 1: 1, last - 1: 2, last: 3}
    slot_two = {first + 2: 4, first + 3: 5, last - 3: 6, last - 2: 7}
    span = lambda a, b: list(range(a, b + 1))
    run(
        read_one,
        vone,
        write_mid,
        span(first + 1, last - 1),
        span(first, last),
        span(first + 2, last - 2),
        span(first + 1, last - 1),
        slot_one,
    )
    run(
        read_two,
        vtwo,
        write_main,
        span(first + 3, last - 3),
        span(first + 2, last - 2),
        span(first + 4, last - 4),
        span(first + 3, last - 3),
        slot_two,
    )

    across.wait_recv()
    for copy in onward:
        copy.start()

    for ns in (0, 1):

        @pl.when(has[ns])
        def _(ns=ns):
            for copy in row_copies(1 - ns):
                copy.wait_recv()

    for ns in (0, 1):
        covered = jnp.where(dry, land_y[ns].astype(jnp.float32), 1.0)
        beyond_mask.append(present[ns] * covered)
    run(
        read_one,
        vone,
        write_mid,
        span(first - 3, first) + span(last, last + 3),
        [first - 2, first - 1, last + 1, last + 2],
        span(first - 2, first + 1) + span(last - 1, last + 2),
        [first - 1, first, last, last + 1],
        slot_one,
    )
    run(
        read_two,
        vtwo,
        write_main,
        span(first - 1, first + 2) + span(last - 2, last + 1),
        [first, first + 1, last - 1, last],
        span(first, first + 3) + span(last - 3, last),
        span(first, first + 2) + span(last - 2, last),
        slot_two,
    )

    own = is_own(levels)

    def place(lower, upper, rest, r, only_own):
        by = SPAN * plan.shift[r]
        jj, blk = by_size[lower.shape[0]]
        a, b = plan.span[r]
        in_west = (blk >= a) & (blk <= b)
        in_east = (blk >= plan.half + a) & (blk <= plan.half + b)
        if only_own:
            in_west, in_east = in_west & (jj >= HALO), in_east & (jj < HALO)
        return jnp.where(
            in_west,
            roll(lower, by),
            jnp.where(in_east, roll(upper, by + SPAN * plan.half), rest),
        )

    beyond_set = [plan.beyond[0][k] % SETS for k in (0, 1)]

    def place_beyond(below, above, k):
        b, t = k, plan.north + k
        size = below.shape[0]
        blk = by_size[size][1]
        both = jnp.where(blk == b, roll(below, SPAN * b + HALO), 0.0)
        both = jnp.where(blk == t, roll(above, SPAN * t + HALO), both)
        turned = roll(both, SPAN * plan.half)
        picked = jnp.where(blk < plan.half, both, turned)
        return jnp.where(is_own(size), picked, 0.0)

    zero = jnp.zeros((levels, cols), jnp.float32)
    zero8 = jnp.zeros((8, cols), jnp.float32)

    def beyond_rows(f):
        rest = [zero] * SETS
        for k in (0, 1):
            rest[beyond_set[k]] = place_beyond(
                ext[f, plan.beyond[0][k]], ext[f, plan.beyond[1][k]], k
            )
        return rest

    rest = [beyond_rows(f) for f in (U, V, PR)]
    rest_mask = [zero8] * SETS
    for k in (0, 1):
        rest_mask[beyond_set[k]] = place_beyond(
            spread(keep(plan.beyond[0][k]), (8, cols)),
            spread(keep(plan.beyond[1][k]), (8, cols)),
            k,
        )
    factor = [None] * SETS
    low_v, high_v = first - 1, last + 1
    for e, flag in ((low_v, present[0]), (high_v, present[1])):
        r = e % SETS
        at = local8 == e // SETS
        factor[r] = jnp.where(at, flag, 1.0 if factor[r] is None else factor[r])
    factor = [None if x is None else stack(x) for x in factor]

    def up(x):
        return [x[1], x[2], roll(x[0], -SPAN)]

    def down(x):
        return [roll(x[2], SPAN), x[0], x[1]]

    cut_low = (block >= plan.half) & (j == 0)
    cut_high = (block < plan.half) & (j == SPAN - 1)

    def strip_step(u, v, p, masks, only_own):
        def span_strip(x):
            ahead, back = roll(x, -1), roll(x, 1)
            change = jnp.where(cut_high, 0.0, ahead) - jnp.where(cut_low, 0.0, back)
            return jnp.where(own, change, 0.0) if only_own else change

        above, under = up(p), down(p)
        v1 = []
        for r in range(SETS):
            value = v[r] - hp * (above[r] - under[r]) - strip_fcor[r] * u[r]
            v1.append(value if factor[r] is None else factor[r] * value)
        u1 = [u[r] + strip_fcor[r] * v[r] - hp * span_strip(p[r]) for r in range(SETS)]
        above, under = up(v1), down(v1)
        p1 = [p[r] - hf * (span_strip(u1[r]) + above[r] - under[r]) for r in range(SETS)]
        p2 = product(p1)
        m = [stack(x) for x in masks]
        return (
            [m[r] * u1[r] for r in range(SETS)],
            [m[r] * v1[r] for r in range(SETS)],
            [m[r] * p2[r] for r in range(SETS)],
        )

    packed = [dense[f] for f in (U, V, PR)]
    strips = [
        [place(packed[f], packed[f], rest[f][r], r, True) for r in range(SETS)]
        for f in (U, V, PR)
    ]
    own_masks = [place(qm, qm, rest_mask[r], r, True) for r in range(SETS)]
    for _ in range(2):
        strips = strip_step(*strips, own_masks, True)
    for f in (U, V, PR):
        for r in range(SETS):
            edge[f, r] = strips[f][r]

    for k in (0, 1):
        sides[k].wait_recv()
    for ns in (0, 1):

        @pl.when(has[ns])
        def _(ns=ns):
            for copy in corner_copies(1 - ns):
                copy.wait_recv()

    got_w, got_e = (side_in[k, pl.ds(0, levels)] for k in (0, 1))
    vw, ve = (side_in[k, pl.ds(levels, mid_level)] for k in (0, 1))
    mw, me = (side_in[k, pl.ds(levels + mid_level, 8)] for k in (0, 1))
    lower = [None] * 3
    upper = [None] * 3
    packed = [dense[f] for f in (U, V, PR)]
    lower[PR] = jnp.where(low, got_w, packed[PR])
    upper[PR] = jnp.where(low, packed[PR], got_e)
    lower[U] = jnp.where(low, roll(got_w, -HALO), packed[U])
    upper[U] = jnp.where(low, packed[U], roll(got_e, HALO))
    lower[V] = jnp.where(
        low, jnp.concatenate([vw, roll(vw, -HALO)], axis=0), packed[V]
    )
    upper[V] = jnp.where(
        low, packed[V], jnp.concatenate([ve, roll(ve, HALO)], axis=0)
    )
    low8 = j8 < HALO
    corners = [[rest[f][r] for r in range(SETS)] for f in (U, V, PR)]
    for k in (0, 1):
        total = corner_in[0, 0]
        blocks = lambda side, ns: functools.reduce(
            jnp.logical_or,
            [
                block8 == (s + plan.corner(side, ns) + 2 * k) % plan.blocks
                for s in SLOTS[:groups]
            ],
        )
        for side, ns in ((0, 1), (1, 0), (1, 1)):
            total = jnp.where(blocks(side, ns), corner_in[side, ns], total)
        at = functools.reduce(
            jnp.logical_or,
            [
                (block == plan.corner(side, ns) + k) & (j // 2 == 1 + side)
                for side in (0, 1)
                for ns in (0, 1)
            ],
        )
        r = beyond_set[k]
        for f in (U, V, PR):
            turned = [roll(total, -SPAN * (SLOTS[g] + k) - turn[f]) for g in range(groups)]
            corners[f][r] = jnp.where(
                at, jnp.concatenate(turned, axis=0), corners[f][r]
            )
    strips = [
        [place(lower[f], upper[f], corners[f][r], r, False) for r in range(SETS)]
        for f in (U, V, PR)
    ]
    lower_mask, upper_mask = jnp.where(low8, mw, qm), jnp.where(low8, qm, me)
    masks = [place(lower_mask, upper_mask, rest_mask[r], r, False) for r in range(SETS)]
    for _ in range(2):
        strips = strip_step(*strips, masks, False)
    high = j >= HALO
    for f in (U, V, PR):
        for r in range(SETS):
            change = strips[f][r] - edge[f, r]
            edge[f, r] = jnp.where(high, change, roll(change, SPAN * plan.half))

    for copy in loads[4:]:
        copy.wait()
    count = count_v[...].astype(jnp.float32)
    match = match_v[...]
    tile = lax.broadcasted_iota(jnp.int32, match.shape, 1)

    def coef(peer):
        mine = jnp.where((tile == lon) & (match == peer), count, 0.0)
        theirs = jnp.where((tile == peer) & (match == lon), count, 0.0)
        chosen = jnp.where(dry, mine, theirs)
        total = jnp.sum(jnp.sum(chosen, axis=1, keepdims=True), axis=0, keepdims=True)
        return spread(total, (rows, cols))

    coefs = [coef(lon), coef(west), coef(east)]
    inverse = KAPPA * mask / (coefs[0] + coefs[1] + coefs[2])
    scaled = [c * inverse for c in coefs]
    for copy in onward:
        copy.wait_recv()
    for f in (U, V, PR):
        value = -KAPPA * mask * own_s[f]
        for k in range(3):
            value = value + scaled[k] * surf[k, f]
        flux[f] = value

    for copy in sides + [across] + onward:
        copy.wait_send()
    for ns in (0, 1):

        @pl.when(has[ns])
        def _(ns=ns):
            for copy in corner_copies(ns) + row_copies(ns):
                copy.wait_send()


def finish(sizes, main, edge, flux, out, held, sem):
    levels, rows, cols = sizes
    plan = Layout(rows, cols)
    lane = lax.broadcasted_iota(jnp.int32, (levels, cols), 1)
    near = (lane < HALO) | (lane >= cols - HALO)
    top = lax.broadcasted_iota(jnp.int32, (8, cols), 0) == 0
    for y in range(rows):
        e = y + HALO
        by = (-SPAN * (e // SETS) - HALO) % cols
        for f in (U, V, PR):
            change = pltpu.roll(edge[f, e % SETS], by, 1)
            value = main[f, y] + jnp.where(near, change, 0.0)
            added = jnp.broadcast_to(flux[f, y : y + 1], (8, cols))
            held[f, y, 0:8] = value[0:8] + jnp.where(top, added, 0.0)
            held[f, y, 8:levels] = value[8:]
            pltpu.make_async_copy(held.at[f, y], out.at[f, :, y, :], sem.at[f]).start()
    for f in (U, V, PR):
        pltpu.make_async_copy(held.at[f], held.at[f], sem.at[f]).wait()


def shards(n_lat, n_lon, state, push, fill, vertical, land, match, counts):
    _, fields, levels, rows, cols = state.shape
    assert fields == 3 and levels % 16 == 0 and levels <= 32 and rows >= 16 and n_lon > 2
    f32 = jnp.float32
    any_spec = pl.BlockSpec(memory_space=pl.ANY)
    vmem_spec = pl.BlockSpec(memory_space=pltpu.VMEM)
    tall = rows + 2 * HALO
    line = (levels, cols)
    side_rows = levels + levels // 2 + 8
    main, edge, flux = pl.pallas_call(
        functools.partial(exchange, (levels, rows, cols, n_lat, n_lon)),
        out_shape=[
            pltpu.VMEM((fields, rows) + line, f32),
            pltpu.VMEM((fields, SETS) + line, f32),
            pltpu.VMEM((fields, rows, cols), f32),
        ],
        in_specs=[any_spec] * 7,
        out_specs=[vmem_spec] * 3,
        scratch_shapes=[
            pltpu.VMEM((fields, tall) + line, f32),
            pltpu.VMEM((fields, tall) + line, f32),
            pltpu.VMEM((tall,) + line, f32),
            pltpu.VMEM((tall,) + line, f32),
            pltpu.VMEM((8,) + line, f32),
            pltpu.VMEM((fields,) + line, f32),
            pltpu.VMEM(push.shape, f32),
            pltpu.VMEM(fill.shape, f32),
            pltpu.VMEM(vertical.shape[1:], f32),
            pltpu.VMEM(land.shape, jnp.int32),
            pltpu.VMEM(match.shape[:0:-1], jnp.int32),
            pltpu.VMEM(counts.shape[:0:-1], jnp.int32),
            pltpu.VMEM((fields, rows, cols), f32),
            pltpu.VMEM((2, 8, cols), jnp.int32),
            pltpu.VMEM((2, side_rows, cols), f32),
            pltpu.VMEM((2, side_rows, cols), f32),
            pltpu.VMEM((2, 2, 8, cols), f32),
            pltpu.VMEM((2, 2, 8, cols), f32),
            pltpu.VMEM((3, fields, rows, cols), f32),
            pltpu.SemaphoreType.DMA((10,)),
            pltpu.SemaphoreType.DMA((15,)),
            pltpu.SemaphoreType.DMA((15,)),
        ],
        compiler_params=pltpu.CompilerParams(collective_id=0, has_side_effects=True),
        name="exchange",
    )(
        state[0],
        push,
        fill,
        vertical.reshape(vertical.shape[1:]),
        land,
        match[0].T,
        counts[0].T,
    )
    main, edge, flux = (
        pltpu.with_memory_space_constraint(x, pltpu.VMEM) for x in (main, edge, flux)
    )
    result = pl.pallas_call(
        functools.partial(finish, (levels, rows, cols)),
        out_shape=jax.ShapeDtypeStruct(state.shape[1:], f32),
        in_specs=[vmem_spec] * 3,
        out_specs=any_spec,
        scratch_shapes=[
            pltpu.VMEM((fields, rows) + line, f32),
            pltpu.SemaphoreType.DMA((3,)),
        ],
        name="finish",
    )(main, edge, flux)
    return result[None]


def solution(mesh):
    sizes = dict(mesh.shape)
    return jax.shard_map(
        functools.partial(shards, sizes["lat"], sizes["lon"]),
        mesh=mesh,
        in_specs=(
            P("comp", None, None, "lat", "lon"),
            P("comp", None),
            P("comp", None),
            P("comp", None, None),
            P("lat", "lon"),
            P("lat", None, None),
            P("lat", None, None),
        ),
        out_specs=P("comp", None, None, "lat", "lon"),
        check_vma=False,
    )
```

profile of v0, /device:TPU:0, one launch (start us, length us, event | category | flops | bytes accessed | tf_op | source)
XLA Modules:
  0.0 13.4 jit_solution(310903406387840440)
XLA Ops:
  0.0 12.5 %exchange.1 = (f32[3,16,32,128]{3,2,1,0:T(8,128)S(1)}, f32[3,3,32,128]{3,2,1,0:T(8,128)S(1)}, f32[3,16,128]{2,1,0:T(8,128)S(1)}) custom-call(f32[3,32,16,128]{3,2,1,0:T(8,128)} %bitcast.9, f32[1,32]{1,0:T(1,128)} %push_in.1, f32[1,32]{1,0:T(1,128)} %fill_in.1, f32[32,32]{1,0:T(8,128)} %bitcast.10, s32[16,128]{1,0:T(8,128)} %land_in.1, s32[2,4]{1,0:T(2,128)} %bitcast.11, ...), custom_call_target="tpu_custom_call" | custom-call | tf_op jit(solution)/shard_map/exchange/pallas_call | solution.py:705
  12.5 1.0 %finish.1 = f32[3,32,16,128]{3,2,1,0:T(8,128)} custom-call(f32[3,16,32,128]{3,2,1,0:T(8,128)S(1)} %get-tuple-element.8.main, f32[3,3,32,128]{3,2,1,0:T(8,128)S(1)} %get-tuple-element.9.edge, f32[3,16,128]{2,1,0:T(8,128)S(1)} %get-tuple-element.10.flux), custom_call_target="tpu_custom_call" | custom-call | tf_op jit(solution)/shard_map/finish/pallas_call | solution.py:752
where the time goes:
time: 13.6 us; the launch traced here: 13.4 us
  Pallas kernels  13.4 us (99%)
    pallas_call x1, Pallas kernels, shards(): pl.pallas_call(functools.partial(exchange, (levels, rows, cols, n_lat, n_...  12.5 us
    pallas_call x1, Pallas kernels, shards(): pl.pallas_call(functools.partial(finish, (levels, rows, cols)), out_shape...  0.95 us

commit v1 on v0

--- a/solution.py
+++ b/solution.py
@@ -17,6 +17,7 @@
 ORDER = (1, 0, 2)
 SLOTS = (0, 1, 4, 5)
 U, V, PR = 0, 1, 2
+ROWS = 5
 
 
 class Layout:
@@ -76,16 +77,20 @@
     land_v,
     match_v,
     count_v,
-    own_s,
     land_y,
     side_out,
     side_in,
+    row_out,
+    row_in,
     corner_out,
     corner_in,
     surf,
+    sizer,
     load_sem,
     send_sem,
     recv_sem,
+    west_sem,
+    other_sem,
 ):
     levels, rows, cols, n_lat, n_lon = sizes
     plan = Layout(rows, cols)
@@ -105,14 +110,37 @@
         pl.semaphore_signal(barrier, inc=1, device_id=to, device_id_type=MESH)
 
     greet((comp, lat, west))
-    greet((comp, lat, east))
-    greet((other, lat, lon))
     for ns in (0, 1):
 
         @pl.when(has[ns])
         def _(ns=ns):
-            for there in (west, east, lon):
-                greet((comp, beside[ns], there))
+            greet((comp, beside[ns], lon))
+            greet((comp, beside[ns], west))
+
+    @pl.when(comp == 0)
+    def _():
+        for there in (lon, west, east):
+            greet((other, lat, there))
+
+    count = [flag.astype(jnp.int32) for flag in has]
+    n_beside = count[0] + count[1]
+
+    def enter(extra):
+        pl.semaphore_wait(barrier, 1 + 2 * n_beside + extra)
+
+        def tell(sem, to):
+            pl.semaphore_signal(sem, inc=1, device_id=to, device_id_type=MESH)
+
+        tell(west_sem, (comp, lat, east))
+        for ns in (0, 1):
+
+            @pl.when(has[ns])
+            def _(ns=ns):
+                tell(west_sem, (comp, beside[ns], east))
+
+        if extra:
+            for there in (lon, west, east):
+                tell(other_sem, (other, lat, there))
 
     small = (
         (push_in, push_v),
@@ -121,21 +149,20 @@
         (land_in, land_v),
         (match_in, match_v),
         (count_in, count_v),
-        (state.at[:, 0], own_s),
     )
     first = HALO
     last = HALO + rows - 1
-    for f in (PR, U, V):
-        for y in range(rows):
-            pltpu.make_async_copy(
-                state.at[f, :, y, :], ext.at[f, first + y], load_sem.at[f]
-            ).start()
     loads = [
         pltpu.make_async_copy(src, dst, load_sem.at[3 + k])
         for k, (src, dst) in enumerate(small)
     ]
     for copy in loads:
         copy.start()
+    for f in (PR, U, V):
+        for y in range(rows):
+            pltpu.make_async_copy(
+                state.at[f, :, y, :], ext.at[f, first + y], load_sem.at[f]
+            ).start()
 
     def wait_field(f):
         own = ext.at[f, pl.ds(first, rows)]
@@ -145,22 +172,10 @@
 
         @pl.when(jnp.logical_not(has[ns]))
         def _(ns=ns):
-            start = 0 if ns == 0 else first + rows
-            for f in (U, V, PR):
-                ext[f, pl.ds(start, HALO)] = jnp.zeros((HALO, levels, cols), jnp.float32)
+            row_in[ns] = jnp.zeros(row_in.shape[1:], jnp.float32)
             land_y[ns] = jnp.zeros((8, cols), jnp.int32)
             for side in (0, 1):
                 corner_in[side, ns] = jnp.zeros((8, cols), jnp.float32)
-
-    @pl.when(has[0])
-    def _():
-        ext[U, 0] = jnp.zeros((levels, cols), jnp.float32)
-        ext[V, 0] = jnp.zeros((levels, cols), jnp.float32)
-
-    @pl.when(has[1])
-    def _():
-        ext[U, last + HALO] = jnp.zeros((levels, cols), jnp.float32)
-        ext[V, last + HALO] = jnp.zeros((levels, cols), jnp.float32)
 
     present = [flag.astype(jnp.float32) for flag in has]
     lane = lax.broadcasted_iota(jnp.int32, (levels, cols), 1)
@@ -190,6 +205,57 @@
     def roll(x, by):
         by = by % cols
         return pltpu.roll(x, by, 1) if by else x
+
+    def remote(src, dst, sent, got, to):
+        return pltpu.make_async_remote_copy(
+            src_ref=src,
+            dst_ref=dst,
+            send_sem=send_sem.at[sent],
+            recv_sem=recv_sem.at[got],
+            device_id=to,
+            device_id_type=MESH,
+        )
+
+    def side_copy(k, to):
+        return remote(side_out.at[k], side_in.at[k], 0, 0, (comp, lat, to))
+
+    sides = [side_copy(0, east), side_copy(1, west)]
+
+    def corner_copy(ns, side):
+        return remote(
+            corner_out.at[ns, side],
+            corner_in.at[side, 1 - ns],
+            1 + ns,
+            1 + (1 - ns),
+            (comp, beside[ns], (east, west)[side]),
+        )
+
+    def row_copies(ns):
+        its = 1 - ns
+        to = (comp, beside[ns], lon)
+        start = 0 if ns == 0 else rows - 8
+        return [
+            remote(row_out.at[ns], row_in.at[its], 1 + ns, 3 + its, to),
+            remote(land_in.at[pl.ds(start, 8)], land_y.at[its], 1 + ns, 3 + its, to),
+        ]
+
+    across = [
+        remote(state.at[:, 0], surf.at[k], 0, 5, (other, lat, there))
+        for k, there in enumerate((lon, east, west))
+    ]
+
+    side_size = side_out.shape[1]
+    row_size = row_out.shape[1] + 8
+
+    def wait_for(sem, size):
+        view = sizer.at[pl.ds(0, size)]
+        pltpu.make_async_copy(view, view, sem).wait()
+
+    @pl.when(comp == 1)
+    def _():
+        enter(3)
+        for copy in across:
+            copy.start()
 
     def pack(row):
         result = None
@@ -201,31 +267,53 @@
         return result
 
     def pack_field(f):
-        wait_field(f)
         packed = pack(lambda y: ext[f, first + y])
         dense[f] = packed
         return packed
 
-    low = j < HALO
-    qp = pack_field(PR)
-    qu = pack_field(U)
-    side_out[0, pl.ds(0, levels)] = jnp.where(low, qp, roll(qu, HALO))
-    side_out[1, pl.ds(0, levels)] = jnp.where(low, roll(qu, -HALO), qp)
-    qv = pack_field(V)
-    mid_level = levels // 2
-    half_low = low[:mid_level]
-    v_low, v_high = qv[:mid_level], qv[mid_level:]
-    side_out[0, pl.ds(levels, mid_level)] = jnp.where(half_low, v_low, roll(v_high, HALO))
-    side_out[1, pl.ds(levels, mid_level)] = jnp.where(half_low, roll(v_high, -HALO), v_low)
     for copy in loads[:4]:
         copy.wait()
     dry = comp == 1
     mask = jnp.where(dry, land_v[...].astype(jnp.float32), 1.0)
     spread = jnp.broadcast_to
-    qm = pack(lambda y: spread(mask[y : y + 1], (8, cols)))
-    side_out[0, pl.ds(levels + mid_level, 8)] = qm
-    side_out[1, pl.ds(levels + mid_level, 8)] = qm
-
+    diag = lax.broadcasted_iota(jnp.int32, (levels, levels), 0) == lax.broadcasted_iota(
+        jnp.int32, (levels, levels), 1
+    )
+
+    def per_level(ref):
+        wide = spread(ref[...], (levels, levels))
+        column = jnp.sum(jnp.where(diag, wide, 0.0), axis=1, keepdims=True)
+        return spread(column * 0.5, (levels, cols))
+
+    hp = per_level(push_v)
+    hf = per_level(fill_v)
+    vert = vert_v[...]
+    vert_hi = vert.astype(jnp.bfloat16).astype(jnp.float32)
+    vert_cat = jnp.concatenate([vert_hi, vert_hi, vert - vert_hi], axis=1).astype(
+        jnp.bfloat16
+    )
+
+    def split(x):
+        hi = x.astype(jnp.bfloat16)
+        lo = (x - hi.astype(jnp.float32)).astype(jnp.bfloat16)
+        return jnp.concatenate([hi, lo, hi], axis=0)
+
+    def product(pieces):
+        result = jnp.dot(
+            vert_cat,
+            jnp.concatenate([split(x) for x in pieces], axis=1),
+            preferred_element_type=jnp.float32,
+        )
+        return [result[:, i * cols : (i + 1) * cols] for i in range(len(pieces))]
+
+    low = j < HALO
+    wait_field(PR)
+    qp = pack_field(PR)
+    wait_field(U)
+    qu = pack_field(U)
+    side_out[0, pl.ds(0, levels)] = jnp.where(low, qp, roll(qu, HALO))
+    side_out[1, pl.ds(0, levels)] = jnp.where(low, roll(qu, -HALO), qp)
+    wait_field(V)
     turn = {PR: 0, U: -2, V: 2}
     for ns in (0, 1):
         its = 1 - ns
@@ -240,118 +328,34 @@
                     piece = roll(value[8 * g : 8 * g + 8], SPAN * b + HALO + turn[f])
                     total = jnp.where(block8 == b, piece, total)
             found[f] = total
+        for f in (U, V, PR):
+            row_out[ns, pl.ds(ROWS * levels + 8 * f, 8)] = found[f]
         to_east = jnp.where(j8 < 2, found[U], jnp.where(j8 < 4, found[PR], found[V]))
         to_west = jnp.where(j8 < 4, found[U], jnp.where(j8 < 6, found[PR], found[V]))
         corner_out[ns, 0] = to_east
         corner_out[ns, 1] = roll(to_west, SPAN * plan.half)
 
-    def remote(src, dst, sent, got, to):
-        return pltpu.make_async_remote_copy(
-            src_ref=src,
-            dst_ref=dst,
-            send_sem=send_sem.at[sent],
-            recv_sem=recv_sem.at[got],
-            device_id=to,
-            device_id_type=MESH,
-        )
-
-    def side_copy(k, to):
-        return remote(side_out.at[k], side_in.at[k], k, k, (comp, lat, to))
-
-    sides = [side_copy(0, east), side_copy(1, west)]
-
-    def corner_copies(ns):
-        return [
-            remote(
-                corner_out.at[ns, side],
-                corner_in.at[side, 1 - ns],
-                2 + 2 * ns + side,
-                2 + 2 * (1 - ns) + side,
-                (comp, beside[ns], (east, west)[side]),
-            )
-            for side in (0, 1)
-        ]
-
-    def row_copies(ns):
-        its = 1 - ns
-        base, peer = 6 + 3 * ns, 6 + 3 * its
-        to = (comp, beside[ns], lon)
-        if ns == 0:
-            p_from, p_to, w_from, w_to = first, first + rows, first, first + rows
-        else:
-            p_from, p_to, w_from, w_to = last + 1 - HALO, 0, last + 2 - HALO, 1
-        return [
-            remote(
-                ext.at[PR, pl.ds(p_from, HALO)],
-                ext.at[PR, pl.ds(p_to, HALO)],
-                base,
-                peer,
-                to,
-            ),
-            remote(
-                ext.at[pl.ds(0, 2), pl.ds(w_from, HALO - 1)],
-                ext.at[pl.ds(0, 2), pl.ds(w_to, HALO - 1)],
-                base + 1,
-                peer + 1,
-                to,
-            ),
-            remote(
-                land_in.at[pl.ds(0 if ns == 0 else rows - 8, 8)],
-                land_y.at[its],
-                base + 2,
-                peer + 2,
-                to,
-            ),
-        ]
-
-    across = remote(state.at[:, 0], surf.at[0], 12, 12, (other, lat, lon))
-    onward = [
-        remote(surf.at[0], surf.at[k], 12 + k, 12 + k, (comp, lat, to))
-        for k, to in ((1, east), (2, west))
-    ]
-
-    count_there = [flag.astype(jnp.int32) for flag in has]
-    pl.semaphore_wait(barrier, 3 + 3 * (count_there[0] + count_there[1]))
-    for copy in reversed(sides):
-        copy.start()
+    @pl.when(comp == 0)
+    def _():
+        enter(0)
+
     for ns in (0, 1):
 
         @pl.when(has[ns])
         def _(ns=ns):
-            for copy in corner_copies(ns) + row_copies(ns):
-                copy.start()
-
-    across.start()
-
-    diag = lax.broadcasted_iota(jnp.int32, (levels, levels), 0) == lax.broadcasted_iota(
-        jnp.int32, (levels, levels), 1
-    )
-
-    def per_level(ref):
-        wide = spread(ref[...], (levels, levels))
-        column = jnp.sum(jnp.where(diag, wide, 0.0), axis=1, keepdims=True)
-        return spread(column * 0.5, (levels, cols))
-
-    hp = per_level(push_v)
-    hf = per_level(fill_v)
-    vert = vert_v[...]
-    vert_hi = vert.astype(jnp.bfloat16).astype(jnp.float32)
-    vert_cat = jnp.concatenate([vert_hi, vert_hi, vert - vert_hi], axis=1).astype(
-        jnp.bfloat16
-    )
-
-    def split(x):
-        hi = x.astype(jnp.bfloat16)
-        lo = (x - hi.astype(jnp.float32)).astype(jnp.bfloat16)
-        return jnp.concatenate([hi, lo, hi], axis=0)
-
-    def product(pieces):
-        result = jnp.dot(
-            vert_cat,
-            jnp.concatenate([split(x) for x in pieces], axis=1),
-            preferred_element_type=jnp.float32,
-        )
-        return [result[:, i * cols : (i + 1) * cols] for i in range(len(pieces))]
+            corner_copy(ns, 0).start()
+
+    qv = pack_field(V)
+    mid_level = levels // 2
+    half_low = low[:mid_level]
+    v_low, v_high = qv[:mid_level], qv[mid_level:]
+    side_out[0, pl.ds(levels, mid_level)] = jnp.where(half_low, v_low, roll(v_high, HALO))
+    side_out[1, pl.ds(levels, mid_level)] = jnp.where(half_low, roll(v_high, -HALO), v_low)
+    qm = pack(lambda y: spread(mask[y : y + 1], (8, cols)))
+    side_out[0, pl.ds(levels + mid_level, 8)] = qm
+    side_out[1, pl.ds(levels + mid_level, 8)] = qm
+
+    sides[0].start()
 
     is_first, is_last = lane == 0, lane == cols - 1
 
@@ -373,10 +377,6 @@
     def advance_v(read, store, es):
         for e in es:
             v1 = read(V, e) - hp * (read(PR, e + 1) - read(PR, e - 1)) - force(e) * read(U, e)
-            if e == first - 1:
-                v1 = present[0] * v1
-            if e == last + 1:
-                v1 = present[1] * v1
             store[e] = v1
 
     def advance_u(read, e):
@@ -419,12 +419,45 @@
     slot_one = {first: 0, first + 1: 1, last - 1: 2, last: 3}
     slot_two = {first + 2: 4, first + 3: 5, last - 3: 6, last - 2: 7}
     span = lambda a, b: list(range(a, b + 1))
+
+    toward = (1.0, -1.0)
+    edges = ((first, first + 1, first + 2), (last, last - 1, last - 2))
+    advance_v(read_one, vone, span(first + 1, first + 2) + span(last - 2, last - 1))
+    for ns in (0, 1):
+        a, b, c = edges[ns]
+        sign = toward[ns]
+        partial = {}
+        for e in (a, b):
+            u1, partial[e] = advance_u(read_one, e)
+            mid[U, e] = keep(e) * u1
+            part[slot_one[e]] = partial[e]
+            if e == a:
+                u_edge = u1
+        w = ext[V, a] - sign * (hp * ext[PR, b]) - force(a) * ext[U, a]
+        sent = (
+            ext[PR, a],
+            w,
+            partial[a] - sign * (hf * vone[b]),
+            partial[b] - sign * (hf * (vone[c] - w)),
+            w - force(a) * u_edge,
+        )
+        for k, value in enumerate(sent):
+            row_out[ns, pl.ds(k * levels, levels)] = value
+
+    for even in (0, 1):
+        for ns in (even, 1 - even):
+
+            @pl.when(has[ns] & (lax.rem(lat, 2) == even))
+            def _(ns=ns):
+                for copy in row_copies(ns):
+                    copy.start()
+
     run(
         read_one,
         vone,
         write_mid,
-        span(first + 1, last - 1),
-        span(first, last),
+        span(first + 3, last - 3),
+        span(first + 2, last - 2),
         span(first + 2, last - 2),
         span(first + 1, last - 1),
         slot_one,
@@ -440,35 +473,61 @@
         slot_two,
     )
 
-    across.wait_recv()
-    for copy in onward:
-        copy.start()
-
+    def send_west():
+        pl.semaphore_wait(west_sem, 1 + n_beside)
+        sides[1].start()
+        for ns in (0, 1):
+
+            @pl.when(has[ns])
+            def _(ns=ns):
+                corner_copy(ns, 1).start()
+
+        @pl.when(comp == 0)
+        def _():
+            pl.semaphore_wait(other_sem, 3)
+            for copy in across:
+                copy.start()
+
+    send_west()
     for ns in (0, 1):
 
         @pl.when(has[ns])
         def _(ns=ns):
-            for copy in row_copies(1 - ns):
-                copy.wait_recv()
+            wait_for(recv_sem.at[3 + ns], row_size)
 
     for ns in (0, 1):
         covered = jnp.where(dry, land_y[ns].astype(jnp.float32), 1.0)
         beyond_mask.append(present[ns] * covered)
-    run(
-        read_one,
-        vone,
-        write_mid,
-        span(first - 3, first) + span(last, last + 3),
-        [first - 2, first - 1, last + 1, last + 2],
-        span(first - 2, first + 1) + span(last - 1, last + 2),
-        [first - 1, first, last, last + 1],
-        slot_one,
-    )
+    def got(ns, k):
+        return row_in[ns, pl.ds(k * levels, levels)]
+
+    ready = {}
+    for ns in (0, 1):
+        r, r2, r3 = edges[ns]
+        a, b = (r - 1, r - 2) if ns == 0 else (r + 1, r + 2)
+        sign = -toward[ns]
+        p_r = ext[PR, r]
+        v_r = ext[V, r] - sign * (hp * (got(ns, 0) - ext[PR, r2])) - force(r) * ext[U, r]
+        v_a = present[ns] * (got(ns, 1) + sign * (hp * p_r))
+        vone[r] = v_r
+        mid[V, r] = keep(r) * v_r
+        ready[r] = part[slot_one[r]] - sign * (hf * (v_a - vone[r2]))
+        ready[r2] = part[slot_one[r2]] - sign * (hf * (v_r - vone[r3]))
+        ready[a] = got(ns, 2) + sign * (hf * v_r)
+        ready[b] = got(ns, 3) + hf * (hp * p_r)
+    for e, value in zip(ready, product(list(ready.values()))):
+        mid[PR, e] = keep(e) * value
+    for ns in (0, 1):
+        r = edges[ns][0]
+        a, b = (r - 1, r - 2) if ns == 0 else (r + 1, r + 2)
+        sign = -toward[ns]
+        own_part = keep(a) * (got(ns, 4) + sign * (hp * ext[PR, r]))
+        vtwo[a] = present[ns] * (own_part - sign * (hp * (mid[PR, b] - mid[PR, r])))
     run(
         read_two,
         vtwo,
         write_main,
-        span(first - 1, first + 2) + span(last - 2, last + 1),
+        span(first, first + 2) + span(last - 2, last),
         [first, first + 1, last - 1, last],
         span(first, first + 3) + span(last - 3, last),
         span(first, first + 2) + span(last - 2, last),
@@ -506,12 +565,30 @@
     zero = jnp.zeros((levels, cols), jnp.float32)
     zero8 = jnp.zeros((8, cols), jnp.float32)
 
+    def slots_of(side, ns, k):
+        return functools.reduce(
+            jnp.logical_or,
+            [
+                block8 == (s + plan.corner(side, ns) + 2 * k) % plan.blocks
+                for s in SLOTS[:groups]
+            ],
+        )
+
+    def unfold(total, f, k):
+        turned = [roll(total, -SPAN * (SLOTS[g] + k) - turn[f]) for g in range(groups)]
+        return jnp.concatenate(turned, axis=0)
+
     def beyond_rows(f):
         rest = [zero] * SETS
+        here = pl.ds(ROWS * levels + 8 * f, 8)
         for k in (0, 1):
-            rest[beyond_set[k]] = place_beyond(
-                ext[f, plan.beyond[0][k]], ext[f, plan.beyond[1][k]], k
-            )
+            total = jnp.where(slots_of(0, 0, k), row_in[0, here], row_in[1, here])
+            both = unfold(total, f, k)
+            turned = roll(both, SPAN * plan.half)
+            at = lax.rem(block, plan.half)
+            picked = jnp.where(block < plan.half, both, turned)
+            flag = ((at == k) | (at == plan.north + k)) & is_own(levels)
+            rest[beyond_set[k]] = jnp.where(flag, picked, 0.0)
         return rest
 
     rest = [beyond_rows(f) for f in (U, V, PR)]
@@ -573,14 +650,32 @@
         for r in range(SETS):
             edge[f, r] = strips[f][r]
 
-    for k in (0, 1):
-        sides[k].wait_recv()
+    for copy in loads[4:]:
+        copy.wait()
+    tiles = count_v[...].astype(jnp.float32)
+    match = match_v[...]
+    tile = lax.broadcasted_iota(jnp.int32, match.shape, 1)
+
+    def coef(peer):
+        mine = jnp.where((tile == lon) & (match == peer), tiles, 0.0)
+        theirs = jnp.where((tile == peer) & (match == lon), tiles, 0.0)
+        chosen = jnp.where(dry, mine, theirs)
+        total = jnp.sum(jnp.sum(chosen, axis=1, keepdims=True), axis=0, keepdims=True)
+        return spread(total, (rows, cols))
+
+    coefs = [coef(lon), coef(west), coef(east)]
+    inverse = KAPPA * mask / (coefs[0] + coefs[1] + coefs[2])
+    scaled = [c * inverse for c in coefs]
+    for f in (U, V, PR):
+        top = ext[f, pl.ds(first, rows), 0, :]
+        flux[f] = -KAPPA * mask * top
+
+    wait_for(recv_sem.at[0], 2 * side_size)
     for ns in (0, 1):
 
         @pl.when(has[ns])
         def _(ns=ns):
-            for copy in corner_copies(1 - ns):
-                copy.wait_recv()
+            wait_for(recv_sem.at[1 + ns], 16)
 
     got_w, got_e = (side_in[k, pl.ds(0, levels)] for k in (0, 1))
     vw, ve = (side_in[k, pl.ds(levels, mid_level)] for k in (0, 1))
@@ -602,15 +697,8 @@
     corners = [[rest[f][r] for r in range(SETS)] for f in (U, V, PR)]
     for k in (0, 1):
         total = corner_in[0, 0]
-        blocks = lambda side, ns: functools.reduce(
-            jnp.logical_or,
-            [
-                block8 == (s + plan.corner(side, ns) + 2 * k) % plan.blocks
-                for s in SLOTS[:groups]
-            ],
-        )
         for side, ns in ((0, 1), (1, 0), (1, 1)):
-            total = jnp.where(blocks(side, ns), corner_in[side, ns], total)
+            total = jnp.where(slots_of(side, ns, k), corner_in[side, ns], total)
         at = functools.reduce(
             jnp.logical_or,
             [
@@ -621,10 +709,7 @@
         )
         r = beyond_set[k]
         for f in (U, V, PR):
-            turned = [roll(total, -SPAN * (SLOTS[g] + k) - turn[f]) for g in range(groups)]
-            corners[f][r] = jnp.where(
-                at, jnp.concatenate(turned, axis=0), corners[f][r]
-            )
+            corners[f][r] = jnp.where(at, unfold(total, f, k), corners[f][r])
     strips = [
         [place(lower[f], upper[f], corners[f][r], r, False) for r in range(SETS)]
         for f in (U, V, PR)
@@ -639,38 +724,19 @@
             change = strips[f][r] - edge[f, r]
             edge[f, r] = jnp.where(high, change, roll(change, SPAN * plan.half))
 
-    for copy in loads[4:]:
-        copy.wait()
-    count = count_v[...].astype(jnp.float32)
-    match = match_v[...]
-    tile = lax.broadcasted_iota(jnp.int32, match.shape, 1)
-
-    def coef(peer):
-        mine = jnp.where((tile == lon) & (match == peer), count, 0.0)
-        theirs = jnp.where((tile == peer) & (match == lon), count, 0.0)
-        chosen = jnp.where(dry, mine, theirs)
-        total = jnp.sum(jnp.sum(chosen, axis=1, keepdims=True), axis=0, keepdims=True)
-        return spread(total, (rows, cols))
-
-    coefs = [coef(lon), coef(west), coef(east)]
-    inverse = KAPPA * mask / (coefs[0] + coefs[1] + coefs[2])
-    scaled = [c * inverse for c in coefs]
-    for copy in onward:
-        copy.wait_recv()
+    wait_for(recv_sem.at[5], 9 * rows)
     for f in (U, V, PR):
-        value = -KAPPA * mask * own_s[f]
+        value = flux[f]
         for k in range(3):
             value = value + scaled[k] * surf[k, f]
         flux[f] = value
 
-    for copy in sides + [across] + onward:
-        copy.wait_send()
+    wait_for(send_sem.at[0], 2 * side_size + 9 * rows)
     for ns in (0, 1):
 
         @pl.when(has[ns])
         def _(ns=ns):
-            for copy in corner_copies(ns) + row_copies(ns):
-                copy.wait_send()
+            wait_for(send_sem.at[1 + ns], row_size + 16)
 
 
 def finish(sizes, main, edge, flux, out, held, sem):
@@ -724,16 +790,20 @@
             pltpu.VMEM(land.shape, jnp.int32),
             pltpu.VMEM(match.shape[:0:-1], jnp.int32),
             pltpu.VMEM(counts.shape[:0:-1], jnp.int32),
-            pltpu.VMEM((fields, rows, cols), f32),
             pltpu.VMEM((2, 8, cols), jnp.int32),
             pltpu.VMEM((2, side_rows, cols), f32),
             pltpu.VMEM((2, side_rows, cols), f32),
+            pltpu.VMEM((2, ROWS * levels + 24, cols), f32),
+            pltpu.VMEM((2, ROWS * levels + 24, cols), f32),
             pltpu.VMEM((2, 2, 8, cols), f32),
             pltpu.VMEM((2, 2, 8, cols), f32),
             pltpu.VMEM((3, fields, rows, cols), f32),
-            pltpu.SemaphoreType.DMA((10,)),
-            pltpu.SemaphoreType.DMA((15,)),
-            pltpu.SemaphoreType.DMA((15,)),
+            pltpu.VMEM((ROWS * levels + 48 + 9 * rows, cols), f32),
+            pltpu.SemaphoreType.DMA((9,)),
+            pltpu.SemaphoreType.DMA((3,)),
+            pltpu.SemaphoreType.DMA((6,)),
+            pltpu.SemaphoreType.REGULAR,
+            pltpu.SemaphoreType.REGULAR,
         ],
         compiler_params=pltpu.CompilerParams(collective_id=0, has_side_effects=True),
         name="exchange",

time: 13.6 us -> 12 us (0.88)
  the two profiles are of different devices: /device:TPU:0 before, /device:TPU:5 now
where the time goes in v1:
time: 12 us; the launch traced here: 11.8 us
  Pallas kernels  11.8 us (98%)
    pallas_call x1, Pallas kernels, shards(): pl.pallas_call(functools.partial(exchange, (levels, rows, cols, n_lat, n_...  10.8 us
    pallas_call x1, Pallas kernels, shards(): pl.pallas_call(functools.partial(finish, (levels, rows, cols)), out_shape...  0.95 us

profile of v1, /device:TPU:5, one launch (start us, length us, event | category | flops | bytes accessed | tf_op | source)
XLA Modules:
  0.0 11.8 jit_solution(6236854018680972978)
XLA Ops:
  0.0 10.8 %exchange.1 = (f32[3,16,32,128]{3,2,1,0:T(8,128)S(1)}, f32[3,3,32,128]{3,2,1,0:T(8,128)S(1)}, f32[3,16,128]{2,1,0:T(8,128)S(1)}) custom-call(f32[3,32,16,128]{3,2,1,0:T(8,128)} %bitcast.9, f32[1,32]{1,0:T(1,128)} %push_in.1, f32[1,32]{1,0:T(1,128)} %fill_in.1, f32[32,32]{1,0:T(8,128)} %bitcast.10, s32[16,128]{1,0:T(8,128)} %land_in.1, s32[2,4]{1,0:T(2,128)} %bitcast.11, ...), custom_call_target="tpu_custom_call" | custom-call | tf_op jit(solution)/shard_map/exchange/pallas_call | solution.py:771
  10.8 1.0 %finish.1 = f32[3,32,16,128]{3,2,1,0:T(8,128)} custom-call(f32[3,16,32,128]{3,2,1,0:T(8,128)S(1)} %get-tuple-element.8.main, f32[3,3,32,128]{3,2,1,0:T(8,128)S(1)} %get-tuple-element.9.edge, f32[3,16,128]{2,1,0:T(8,128)S(1)} %get-tuple-element.10.flux), custom_call_target="tpu_custom_call" | custom-call | tf_op jit(solution)/shard_map/finish/pallas_call | solution.py:822

commit v2 on v1

--- a/solution.py
+++ b/solution.py
@@ -89,7 +89,7 @@
     load_sem,
     send_sem,
     recv_sem,
-    west_sem,
+    told_sem,
     other_sem,
 ):
     levels, rows, cols, n_lat, n_lon = sizes
@@ -109,38 +109,52 @@
     def greet(to):
         pl.semaphore_signal(barrier, inc=1, device_id=to, device_id_type=MESH)
 
-    greet((comp, lat, west))
+    beside_x = (east, west)
+    early = (lon == n_lon - 1, lon > 0)
+    count = [flag.astype(jnp.int32) for flag in has]
+    n_beside = count[0] + count[1]
+    n_early = early[0].astype(jnp.int32) + early[1].astype(jnp.int32)
+
+    def every(there, sem):
+        def tell(to):
+            pl.semaphore_signal(sem, inc=1, device_id=to, device_id_type=MESH)
+
+        tell((comp, lat, there))
+        tell((other, lat, there))
+        for ns in (0, 1):
+
+            @pl.when(has[ns])
+            def _(ns=ns):
+                tell((comp, beside[ns], there))
+
+    for d in (0, 1):
+
+        @pl.when(jnp.logical_not(early[d]))
+        def _(d=d):
+            every(beside_x[d], barrier)
+
     for ns in (0, 1):
 
         @pl.when(has[ns])
         def _(ns=ns):
             greet((comp, beside[ns], lon))
-            greet((comp, beside[ns], west))
 
     @pl.when(comp == 0)
     def _():
-        for there in (lon, west, east):
-            greet((other, lat, there))
-
-    count = [flag.astype(jnp.int32) for flag in has]
-    n_beside = count[0] + count[1]
+        greet((other, lat, lon))
 
     def enter(extra):
-        pl.semaphore_wait(barrier, 1 + 2 * n_beside + extra)
-
-        def tell(sem, to):
-            pl.semaphore_signal(sem, inc=1, device_id=to, device_id_type=MESH)
-
-        tell(west_sem, (comp, lat, east))
-        for ns in (0, 1):
-
-            @pl.when(has[ns])
-            def _(ns=ns):
-                tell(west_sem, (comp, beside[ns], east))
+        pl.semaphore_wait(barrier, n_beside + n_early * (2 + n_beside) + extra)
+        for d in (0, 1):
+
+            @pl.when(early[d])
+            def _(d=d):
+                every(beside_x[d], told_sem)
 
         if extra:
-            for there in (lon, west, east):
-                tell(other_sem, (other, lat, there))
+            pl.semaphore_signal(
+                other_sem, inc=1, device_id=(other, lat, lon), device_id_type=MESH
+            )
 
     small = (
         (push_in, push_v),
@@ -253,9 +267,14 @@
 
     @pl.when(comp == 1)
     def _():
-        enter(3)
-        for copy in across:
-            copy.start()
+        enter(1)
+        for d in (0, 1):
+
+            @pl.when(early[d])
+            def _(d=d):
+                across[1 + d].start()
+
+        across[0].start()
 
     def pack(row):
         result = None
@@ -339,11 +358,18 @@
     def _():
         enter(0)
 
-    for ns in (0, 1):
-
-        @pl.when(has[ns])
-        def _(ns=ns):
-            corner_copy(ns, 0).start()
+    def send_corners(d):
+        for ns in (0, 1):
+
+            @pl.when(has[ns])
+            def _(ns=ns):
+                corner_copy(ns, d).start()
+
+    for d in (0, 1):
+
+        @pl.when(early[d])
+        def _(d=d):
+            send_corners(d)
 
     qv = pack_field(V)
     mid_level = levels // 2
@@ -355,7 +381,11 @@
     side_out[0, pl.ds(levels + mid_level, 8)] = qm
     side_out[1, pl.ds(levels + mid_level, 8)] = qm
 
-    sides[0].start()
+    for d in (0, 1):
+
+        @pl.when(early[d])
+        def _(d=d):
+            sides[d].start()
 
     is_first, is_last = lane == 0, lane == cols - 1
 
@@ -473,22 +503,28 @@
         slot_two,
     )
 
-    def send_west():
-        pl.semaphore_wait(west_sem, 1 + n_beside)
-        sides[1].start()
-        for ns in (0, 1):
-
-            @pl.when(has[ns])
-            def _(ns=ns):
-                corner_copy(ns, 1).start()
-
-        @pl.when(comp == 0)
-        def _():
-            pl.semaphore_wait(other_sem, 3)
-            for copy in across:
-                copy.start()
-
-    send_west()
+    @pl.when(n_early < 2)
+    def _():
+        pl.semaphore_wait(told_sem, (2 - n_early) * (2 + n_beside))
+
+    for d in (0, 1):
+
+        @pl.when(jnp.logical_not(early[d]))
+        def _(d=d):
+            sides[d].start()
+            send_corners(d)
+
+    for d in (0, 1):
+
+        @pl.when(jnp.logical_not(early[d]) | (comp == 0))
+        def _(d=d):
+            across[1 + d].start()
+
+    @pl.when(comp == 0)
+    def _():
+        pl.semaphore_wait(other_sem, 1)
+        across[0].start()
+
     for ns in (0, 1):
 
         @pl.when(has[ns])

time: 12 us -> 11.3 us (0.942)
  the two profiles are of different devices: /device:TPU:5 before, /device:TPU:25 now
where the time goes in v2:
time: 11.3 us; the launch traced here: 11.1 us
  Pallas kernels  11.1 us (98%)
    pallas_call x1, Pallas kernels, shards(): pl.pallas_call(functools.partial(exchange, (levels, rows, cols, n_lat, n_...  10.2 us
    pallas_call x1, Pallas kernels, shards(): pl.pallas_call(functools.partial(finish, (levels, rows, cols)), out_shape...  0.95 us

profile of v2, /device:TPU:25, one launch (start us, length us, event | category | flops | bytes accessed | tf_op | source)
XLA Modules:
  0.0 11.1 jit_solution(1612782624869453201)
XLA Ops:
  0.0 10.2 %exchange.1 = (f32[3,16,32,128]{3,2,1,0:T(8,128)S(1)}, f32[3,3,32,128]{3,2,1,0:T(8,128)S(1)}, f32[3,16,128]{2,1,0:T(8,128)S(1)}) custom-call(f32[3,32,16,128]{3,2,1,0:T(8,128)} %bitcast.9, f32[1,32]{1,0:T(1,128)} %push_in.1, f32[1,32]{1,0:T(1,128)} %fill_in.1, f32[32,32]{1,0:T(8,128)} %bitcast.10, s32[16,128]{1,0:T(8,128)} %land_in.1, s32[2,4]{1,0:T(2,128)} %bitcast.11, ...), custom_call_target="tpu_custom_call" | custom-call | tf_op jit(solution)/shard_map/exchange/pallas_call | solution.py:807
  10.2 1.0 %finish.1 = f32[3,32,16,128]{3,2,1,0:T(8,128)} custom-call(f32[3,16,32,128]{3,2,1,0:T(8,128)S(1)} %get-tuple-element.8.main, f32[3,3,32,128]{3,2,1,0:T(8,128)S(1)} %get-tuple-element.9.edge, f32[3,16,128]{2,1,0:T(8,128)S(1)} %get-tuple-element.10.flux), custom_call_target="tpu_custom_call" | custom-call | tf_op jit(solution)/shard_map/finish/pallas_call | solution.py:858

commit v3 on v2

--- a/solution.py
+++ b/solution.py
@@ -71,6 +71,7 @@
     vtwo,
     part,
     dense,
+    strip,
     push_v,
     fill_v,
     vert_v,
@@ -149,7 +150,7 @@
 
             @pl.when(early[d])
             def _(d=d):
-                every(beside_x[d], told_sem)
+                every(beside_x[d], told_sem.at[1 - d])
 
         if extra:
             pl.semaphore_signal(
@@ -197,7 +198,12 @@
     j, block = lax.rem(lane, SPAN), lane // SPAN
     j8, block8 = lax.rem(lane8, SPAN), lane8 // SPAN
     west8 = block8 < plan.half
-    by_size = {levels: (j, block), 8: (j8, block8)}
+    half_lane = lane[: levels // 2]
+    by_size = {
+        levels: (j, block),
+        levels // 2: (lax.rem(half_lane, SPAN), half_lane // SPAN),
+        8: (j8, block8),
+    }
 
     def is_own(size):
         jj, blk = by_size[size]
@@ -325,16 +331,31 @@
         )
         return [result[:, i * cols : (i + 1) * cols] for i in range(len(pieces))]
 
+    qm = pack(lambda y: spread(mask[y : y + 1], (8, cols)))
     low = j < HALO
     wait_field(PR)
     qp = pack_field(PR)
     wait_field(U)
     qu = pack_field(U)
-    side_out[0, pl.ds(0, levels)] = jnp.where(low, qp, roll(qu, HALO))
-    side_out[1, pl.ds(0, levels)] = jnp.where(low, roll(qu, -HALO), qp)
-    wait_field(V)
+    across_by = SPAN * plan.half
+    u_east = jnp.where(j == 0, stack(roll(qm, -2)), qu)
+    u_west = jnp.where(j == SPAN - 1, stack(roll(qm, 3)), qu)
+    side_out[0, pl.ds(0, levels)] = jnp.where(low, qp, roll(u_east, HALO))
+    side_out[1, pl.ds(0, levels)] = jnp.where(
+        low, roll(u_west, across_by + HALO), roll(qp, across_by)
+    )
+    @pl.when(comp == 0)
+    def _():
+        enter(0)
+
     turn = {PR: 0, U: -2, V: 2}
-    for ns in (0, 1):
+
+    def send_corner(ns, d):
+        @pl.when(has[ns])
+        def _():
+            corner_copy(ns, d).start()
+
+    def corner(ns):
         its = 1 - ns
         picked = (0, 1) if ns == 0 else (rows - 2, rows - 1)
         found = {}
@@ -352,40 +373,37 @@
         to_east = jnp.where(j8 < 2, found[U], jnp.where(j8 < 4, found[PR], found[V]))
         to_west = jnp.where(j8 < 4, found[U], jnp.where(j8 < 6, found[PR], found[V]))
         corner_out[ns, 0] = to_east
-        corner_out[ns, 1] = roll(to_west, SPAN * plan.half)
-
-    @pl.when(comp == 0)
-    def _():
-        enter(0)
-
-    def send_corners(d):
-        for ns in (0, 1):
-
-            @pl.when(has[ns])
-            def _(ns=ns):
-                corner_copy(ns, d).start()
-
-    for d in (0, 1):
-
-        @pl.when(early[d])
-        def _(d=d):
-            send_corners(d)
-
+        corner_out[ns, 1] = roll(to_west, across_by)
+        for d in (0, 1):
+
+            @pl.when(early[d])
+            def _(d=d):
+                send_corner(ns, d)
+
+    wait_field(V)
+    corner(0)
     qv = pack_field(V)
     mid_level = levels // 2
     half_low = low[:mid_level]
-    v_low, v_high = qv[:mid_level], qv[mid_level:]
-    side_out[0, pl.ds(levels, mid_level)] = jnp.where(half_low, v_low, roll(v_high, HALO))
-    side_out[1, pl.ds(levels, mid_level)] = jnp.where(half_low, roll(v_high, -HALO), v_low)
-    qm = pack(lambda y: spread(mask[y : y + 1], (8, cols)))
-    side_out[0, pl.ds(levels + mid_level, 8)] = qm
-    side_out[1, pl.ds(levels + mid_level, 8)] = qm
+    v_east = jnp.where(j == 0, stack(roll(qm, -3)), qv)
+    v_west = jnp.where(j == SPAN - 1, stack(roll(qm, 2)), qv)
+    side_out[0, pl.ds(levels, mid_level)] = jnp.where(
+        half_low, v_east[:mid_level], roll(v_east[mid_level:], HALO)
+    )
+    side_out[1, pl.ds(levels, mid_level)] = jnp.where(
+        half_low,
+        roll(v_west[mid_level:], across_by + HALO),
+        roll(v_west[:mid_level], across_by),
+    )
 
     for d in (0, 1):
 
         @pl.when(early[d])
         def _(d=d):
             sides[d].start()
+
+    corner(1)
+
 
     is_first, is_last = lane == 0, lane == cols - 1
 
@@ -503,16 +521,14 @@
         slot_two,
     )
 
-    @pl.when(n_early < 2)
-    def _():
-        pl.semaphore_wait(told_sem, (2 - n_early) * (2 + n_beside))
-
     for d in (0, 1):
 
         @pl.when(jnp.logical_not(early[d]))
         def _(d=d):
+            pl.semaphore_wait(told_sem.at[d], 2 + n_beside)
             sides[d].start()
-            send_corners(d)
+            for ns in (0, 1):
+                send_corner(ns, d)
 
     for d in (0, 1):
 
@@ -572,19 +588,15 @@
 
     own = is_own(levels)
 
-    def place(lower, upper, rest, r, only_own):
-        by = SPAN * plan.shift[r]
-        jj, blk = by_size[lower.shape[0]]
+    def place(packed, rest, r, by, ours):
+        jj, blk = by_size[packed.shape[0]]
         a, b = plan.span[r]
         in_west = (blk >= a) & (blk <= b)
         in_east = (blk >= plan.half + a) & (blk <= plan.half + b)
-        if only_own:
-            in_west, in_east = in_west & (jj >= HALO), in_east & (jj < HALO)
-        return jnp.where(
-            in_west,
-            roll(lower, by),
-            jnp.where(in_east, roll(upper, by + SPAN * plan.half), rest),
-        )
+        lower = jj >= HALO if ours else jj < HALO
+        upper = jj < HALO if ours else jj >= HALO
+        flag = (in_west & lower) | (in_east & upper)
+        return jnp.where(flag, roll(packed, SPAN * plan.shift[r] + by), rest)
 
     beyond_set = [plan.beyond[0][k] % SETS for k in (0, 1)]
 
@@ -674,12 +686,15 @@
             [m[r] * p2[r] for r in range(SETS)],
         )
 
-    packed = [dense[f] for f in (U, V, PR)]
-    strips = [
-        [place(packed[f], packed[f], rest[f][r], r, True) for r in range(SETS)]
-        for f in (U, V, PR)
-    ]
-    own_masks = [place(qm, qm, rest_mask[r], r, True) for r in range(SETS)]
+    low8 = j8 < HALO
+    for f in (U, V, PR):
+        packed = dense[f]
+        packed = jnp.where(low, roll(packed, across_by), packed)
+        for r in range(SETS):
+            strip[f, r] = place(packed, rest[f][r], r, 0, True)
+    packed = jnp.where(low8, roll(qm, across_by), qm)
+    own_masks = [place(packed, rest_mask[r], r, 0, True) for r in range(SETS)]
+    strips = [[strip[f, r] for r in range(SETS)] for f in (U, V, PR)]
     for _ in range(2):
         strips = strip_step(*strips, own_masks, True)
     for f in (U, V, PR):
@@ -715,22 +730,7 @@
 
     got_w, got_e = (side_in[k, pl.ds(0, levels)] for k in (0, 1))
     vw, ve = (side_in[k, pl.ds(levels, mid_level)] for k in (0, 1))
-    mw, me = (side_in[k, pl.ds(levels + mid_level, 8)] for k in (0, 1))
-    lower = [None] * 3
-    upper = [None] * 3
-    packed = [dense[f] for f in (U, V, PR)]
-    lower[PR] = jnp.where(low, got_w, packed[PR])
-    upper[PR] = jnp.where(low, packed[PR], got_e)
-    lower[U] = jnp.where(low, roll(got_w, -HALO), packed[U])
-    upper[U] = jnp.where(low, packed[U], roll(got_e, HALO))
-    lower[V] = jnp.where(
-        low, jnp.concatenate([vw, roll(vw, -HALO)], axis=0), packed[V]
-    )
-    upper[V] = jnp.where(
-        low, packed[V], jnp.concatenate([ve, roll(ve, HALO)], axis=0)
-    )
-    low8 = j8 < HALO
-    corners = [[rest[f][r] for r in range(SETS)] for f in (U, V, PR)]
+    corners = [[strip[f, r] for r in range(SETS)] for f in (U, V, PR)]
     for k in (0, 1):
         total = corner_in[0, 0]
         for side, ns in ((0, 1), (1, 0), (1, 1)):
@@ -746,19 +746,34 @@
         r = beyond_set[k]
         for f in (U, V, PR):
             corners[f][r] = jnp.where(at, unfold(total, f, k), corners[f][r])
+    p_all = jnp.where(low, got_w, got_e)
+    u_all = jnp.where(low, got_e, got_w)
+    v_some = jnp.where(half_low, vw, ve)
+    v_rest = jnp.where(half_low, ve, vw)
     strips = [
-        [place(lower[f], upper[f], corners[f][r], r, False) for r in range(SETS)]
-        for f in (U, V, PR)
+        [place(u_all, corners[U][r], r, -HALO, False) for r in range(SETS)],
+        [
+            jnp.concatenate(
+                [
+                    place(v_some, corners[V][r][:mid_level], r, 0, False),
+                    place(v_rest, corners[V][r][mid_level:], r, -HALO, False),
+                ],
+                axis=0,
+            )
+            for r in range(SETS)
+        ],
+        [place(p_all, corners[PR][r], r, 0, False) for r in range(SETS)],
     ]
-    lower_mask, upper_mask = jnp.where(low8, mw, qm), jnp.where(low8, qm, me)
-    masks = [place(lower_mask, upper_mask, rest_mask[r], r, False) for r in range(SETS)]
+    mask_w = jnp.where(j8 == 2, roll(got_w[:8], -2), roll(vw[:8], 3))
+    mask_e = jnp.where(j8 == HALO, roll(got_e[:8], -7), roll(ve[:8], -2))
+    mask_all = jnp.where(low8, mask_w, mask_e)
+    masks = [place(mask_all, own_masks[r], r, 0, False) for r in range(SETS)]
     for _ in range(2):
         strips = strip_step(*strips, masks, False)
-    high = j >= HALO
     for f in (U, V, PR):
         for r in range(SETS):
             change = strips[f][r] - edge[f, r]
-            edge[f, r] = jnp.where(high, change, roll(change, SPAN * plan.half))
+            edge[f, r] = jnp.where(low, roll(change, across_by), change)
 
     wait_for(recv_sem.at[5], 9 * rows)
     for f in (U, V, PR):
@@ -783,9 +798,9 @@
     top = lax.broadcasted_iota(jnp.int32, (8, cols), 0) == 0
     for y in range(rows):
         e = y + HALO
-        by = (-SPAN * (e // SETS) - HALO) % cols
+        by = -SPAN * (e // SETS) - HALO
         for f in (U, V, PR):
-            change = pltpu.roll(edge[f, e % SETS], by, 1)
+            change = pltpu.roll(edge[f, e % SETS], by % cols, 1)
             value = main[f, y] + jnp.where(near, change, 0.0)
             added = jnp.broadcast_to(flux[f, y : y + 1], (8, cols))
             held[f, y, 0:8] = value[0:8] + jnp.where(top, added, 0.0)
@@ -803,7 +818,7 @@
     vmem_spec = pl.BlockSpec(memory_space=pltpu.VMEM)
     tall = rows + 2 * HALO
     line = (levels, cols)
-    side_rows = levels + levels // 2 + 8
+    side_rows = levels + levels // 2
     main, edge, flux = pl.pallas_call(
         functools.partial(exchange, (levels, rows, cols, n_lat, n_lon)),
         out_shape=[
@@ -820,6 +835,7 @@
             pltpu.VMEM((tall,) + line, f32),
             pltpu.VMEM((8,) + line, f32),
             pltpu.VMEM((fields,) + line, f32),
+            pltpu.VMEM((fields, SETS) + line, f32),
             pltpu.VMEM(push.shape, f32),
             pltpu.VMEM(fill.shape, f32),
             pltpu.VMEM(vertical.shape[1:], f32),
@@ -838,7 +854,7 @@
             pltpu.SemaphoreType.DMA((9,)),
             pltpu.SemaphoreType.DMA((3,)),
             pltpu.SemaphoreType.DMA((6,)),
-            pltpu.SemaphoreType.REGULAR,
+            pltpu.SemaphoreType.REGULAR((2,)),
             pltpu.SemaphoreType.REGULAR,
         ],
         compiler_params=pltpu.CompilerParams(collective_id=0, has_side_effects=True),

time: 11.3 us -> 10.9 us (0.965)
  the two profiles are of different devices: /device:TPU:25 before, /device:TPU:0 now
where the time goes in v3:
time: 10.9 us; the launch traced here: 10.7 us
  Pallas kernels  10.7 us (98%)
    pallas_call x1, Pallas kernels, shards(): pl.pallas_call(functools.partial(exchange, (levels, rows, cols, n_lat, n_...  9.79 us
    pallas_call x1, Pallas kernels, shards(): pl.pallas_call(functools.partial(finish, (levels, rows, cols)), out_shape...  0.95 us

profile of v3, /device:TPU:0, one launch (start us, length us, event | category | flops | bytes accessed | tf_op | source)
XLA Modules:
  0.0 10.7 jit_solution(5758756557316689713)
XLA Ops:
  0.0 9.8 %exchange.1 = (f32[3,16,32,128]{3,2,1,0:T(8,128)S(1)}, f32[3,3,32,128]{3,2,1,0:T(8,128)S(1)}, f32[3,16,128]{2,1,0:T(8,128)S(1)}) custom-call(f32[3,32,16,128]{3,2,1,0:T(8,128)} %bitcast.9, f32[1,32]{1,0:T(1,128)} %push_in.1, f32[1,32]{1,0:T(1,128)} %fill_in.1, f32[32,32]{1,0:T(8,128)} %bitcast.10, s32[16,128]{1,0:T(8,128)} %land_in.1, s32[2,4]{1,0:T(2,128)} %bitcast.11, ...), custom_call_target="tpu_custom_call" | custom-call | tf_op jit(solution)/shard_map/exchange/pallas_call | solution.py:822
  9.8 1.0 %finish.1 = f32[3,32,16,128]{3,2,1,0:T(8,128)} custom-call(f32[3,16,32,128]{3,2,1,0:T(8,128)S(1)} %get-tuple-element.8.main, f32[3,3,32,128]{3,2,1,0:T(8,128)S(1)} %get-tuple-element.9.edge, f32[3,16,128]{2,1,0:T(8,128)S(1)} %get-tuple-element.10.flux), custom_call_target="tpu_custom_call" | custom-call | tf_op jit(solution)/shard_map/finish/pallas_call | solution.py:874

commit v4 on v3

--- a/solution.py
+++ b/solution.py
@@ -105,63 +105,11 @@
     has = (lat > 0, lat < n_lat - 1)
     beside = (lat - 1, lat + 1)
 
-    barrier = pltpu.get_barrier_semaphore()
-
-    def greet(to):
-        pl.semaphore_signal(barrier, inc=1, device_id=to, device_id_type=MESH)
-
-    beside_x = (east, west)
-    early = (lon == n_lon - 1, lon > 0)
-    count = [flag.astype(jnp.int32) for flag in has]
-    n_beside = count[0] + count[1]
-    n_early = early[0].astype(jnp.int32) + early[1].astype(jnp.int32)
-
-    def every(there, sem):
-        def tell(to):
-            pl.semaphore_signal(sem, inc=1, device_id=to, device_id_type=MESH)
-
-        tell((comp, lat, there))
-        tell((other, lat, there))
-        for ns in (0, 1):
-
-            @pl.when(has[ns])
-            def _(ns=ns):
-                tell((comp, beside[ns], there))
-
-    for d in (0, 1):
-
-        @pl.when(jnp.logical_not(early[d]))
-        def _(d=d):
-            every(beside_x[d], barrier)
-
-    for ns in (0, 1):
-
-        @pl.when(has[ns])
-        def _(ns=ns):
-            greet((comp, beside[ns], lon))
-
-    @pl.when(comp == 0)
-    def _():
-        greet((other, lat, lon))
-
-    def enter(extra):
-        pl.semaphore_wait(barrier, n_beside + n_early * (2 + n_beside) + extra)
-        for d in (0, 1):
-
-            @pl.when(early[d])
-            def _(d=d):
-                every(beside_x[d], told_sem.at[1 - d])
-
-        if extra:
-            pl.semaphore_signal(
-                other_sem, inc=1, device_id=(other, lat, lon), device_id_type=MESH
-            )
-
     small = (
+        (land_in, land_v),
         (push_in, push_v),
         (fill_in, fill_v),
         (vert_in, vert_v),
-        (land_in, land_v),
         (match_in, match_v),
         (count_in, count_v),
     )
@@ -171,13 +119,73 @@
         pltpu.make_async_copy(src, dst, load_sem.at[3 + k])
         for k, (src, dst) in enumerate(small)
     ]
-    for copy in loads:
-        copy.start()
-    for f in (PR, U, V):
+
+    def load_field(f):
         for y in range(rows):
             pltpu.make_async_copy(
                 state.at[f, :, y, :], ext.at[f, first + y], load_sem.at[f]
             ).start()
+
+    loads[0].start()
+    load_field(PR)
+
+    barrier = pltpu.get_barrier_semaphore()
+
+    def greet(to):
+        pl.semaphore_signal(barrier, inc=1, device_id=to, device_id_type=MESH)
+
+    beside_x = (east, west)
+    early = (lon == n_lon - 1, lon > 0)
+    soon = (early[0], early[1] & (lon < n_lon - 1))
+    count = [flag.astype(jnp.int32) for flag in has]
+    n_beside = count[0] + count[1]
+    n_early = early[0].astype(jnp.int32) + early[1].astype(jnp.int32)
+
+    def every(there, sem):
+        def tell(to):
+            pl.semaphore_signal(sem, inc=1, device_id=to, device_id_type=MESH)
+
+        tell((comp, lat, there))
+        tell((other, lat, there))
+        for ns in (0, 1):
+
+            @pl.when(has[ns])
+            def _(ns=ns):
+                tell((comp, beside[ns], there))
+
+    for d in (0, 1):
+
+        @pl.when(jnp.logical_not(early[d]))
+        def _(d=d):
+            every(beside_x[d], barrier)
+
+    for ns in (0, 1):
+
+        @pl.when(has[ns])
+        def _(ns=ns):
+            greet((comp, beside[ns], lon))
+
+    @pl.when(comp == 0)
+    def _():
+        greet((other, lat, lon))
+
+    def enter(extra):
+        pl.semaphore_wait(barrier, n_beside + n_early * (2 + n_beside) + extra)
+        for d in (0, 1):
+
+            @pl.when(early[d])
+            def _(d=d):
+                every(beside_x[d], told_sem.at[1 - d])
+
+        if extra:
+            pl.semaphore_signal(
+                other_sem, inc=1, device_id=(other, lat, lon), device_id_type=MESH
+            )
+
+    load_field(U)
+    load_field(V)
+    for copy in loads[1:]:
+        copy.start()
 
     def wait_field(f):
         own = ext.at[f, pl.ds(first, rows)]
@@ -236,10 +244,19 @@
             device_id_type=MESH,
         )
 
-    def side_copy(k, to):
-        return remote(side_out.at[k], side_in.at[k], 0, 0, (comp, lat, to))
-
-    sides = [side_copy(0, east), side_copy(1, west)]
+    def side_copies(k, to):
+        return [
+            remote(
+                side_out.at[k, pl.ds(start, size)],
+                side_in.at[k, pl.ds(start, size)],
+                0,
+                0,
+                (comp, lat, to),
+            )
+            for start, size in ((0, levels), (levels, levels // 2))
+        ]
+
+    sides = [side_copies(0, east), side_copies(1, west)]
 
     def corner_copy(ns, side):
         return remote(
@@ -276,7 +293,7 @@
         enter(1)
         for d in (0, 1):
 
-            @pl.when(early[d])
+            @pl.when(soon[d])
             def _(d=d):
                 across[1 + d].start()
 
@@ -296,41 +313,10 @@
         dense[f] = packed
         return packed
 
-    for copy in loads[:4]:
-        copy.wait()
+    loads[0].wait()
     dry = comp == 1
     mask = jnp.where(dry, land_v[...].astype(jnp.float32), 1.0)
     spread = jnp.broadcast_to
-    diag = lax.broadcasted_iota(jnp.int32, (levels, levels), 0) == lax.broadcasted_iota(
-        jnp.int32, (levels, levels), 1
-    )
-
-    def per_level(ref):
-        wide = spread(ref[...], (levels, levels))
-        column = jnp.sum(jnp.where(diag, wide, 0.0), axis=1, keepdims=True)
-        return spread(column * 0.5, (levels, cols))
-
-    hp = per_level(push_v)
-    hf = per_level(fill_v)
-    vert = vert_v[...]
-    vert_hi = vert.astype(jnp.bfloat16).astype(jnp.float32)
-    vert_cat = jnp.concatenate([vert_hi, vert_hi, vert - vert_hi], axis=1).astype(
-        jnp.bfloat16
-    )
-
-    def split(x):
-        hi = x.astype(jnp.bfloat16)
-        lo = (x - hi.astype(jnp.float32)).astype(jnp.bfloat16)
-        return jnp.concatenate([hi, lo, hi], axis=0)
-
-    def product(pieces):
-        result = jnp.dot(
-            vert_cat,
-            jnp.concatenate([split(x) for x in pieces], axis=1),
-            preferred_element_type=jnp.float32,
-        )
-        return [result[:, i * cols : (i + 1) * cols] for i in range(len(pieces))]
-
     qm = pack(lambda y: spread(mask[y : y + 1], (8, cols)))
     low = j < HALO
     wait_field(PR)
@@ -376,12 +362,22 @@
         corner_out[ns, 1] = roll(to_west, across_by)
         for d in (0, 1):
 
-            @pl.when(early[d])
+            @pl.when(soon[d])
             def _(d=d):
                 send_corner(ns, d)
 
+    for d in (0, 1):
+
+        @pl.when(soon[d])
+        def _(d=d):
+            sides[d][0].start()
+
     wait_field(V)
-    corner(0)
+
+    @pl.when(has[0])
+    def _():
+        corner(0)
+
     qv = pack_field(V)
     mid_level = levels // 2
     half_low = low[:mid_level]
@@ -398,11 +394,46 @@
 
     for d in (0, 1):
 
-        @pl.when(early[d])
+        @pl.when(soon[d])
         def _(d=d):
-            sides[d].start()
-
-    corner(1)
+            sides[d][1].start()
+
+    @pl.when(has[1])
+    def _():
+        corner(1)
+
+    for copy in loads[1:4]:
+        copy.wait()
+
+    diag = lax.broadcasted_iota(jnp.int32, (levels, levels), 0) == lax.broadcasted_iota(
+        jnp.int32, (levels, levels), 1
+    )
+
+    def per_level(ref):
+        wide = spread(ref[...], (levels, levels))
+        column = jnp.sum(jnp.where(diag, wide, 0.0), axis=1, keepdims=True)
+        return spread(column * 0.5, (levels, cols))
+
+    hp = per_level(push_v)
+    hf = per_level(fill_v)
+    vert = vert_v[...]
+    vert_hi = vert.astype(jnp.bfloat16).astype(jnp.float32)
+    vert_cat = jnp.concatenate([vert_hi, vert_hi, vert - vert_hi], axis=1).astype(
+        jnp.bfloat16
+    )
+
+    def split(x):
+        hi = x.astype(jnp.bfloat16)
+        lo = (x - hi.astype(jnp.float32)).astype(jnp.bfloat16)
+        return jnp.concatenate([hi, lo, hi], axis=0)
+
+    def product(pieces):
+        result = jnp.dot(
+            vert_cat,
+            jnp.concatenate([split(x) for x in pieces], axis=1),
+            preferred_element_type=jnp.float32,
+        )
+        return [result[:, i * cols : (i + 1) * cols] for i in range(len(pieces))]
 
 
     is_first, is_last = lane == 0, lane == cols - 1
@@ -492,13 +523,18 @@
         for k, value in enumerate(sent):
             row_out[ns, pl.ds(k * levels, levels)] = value
 
-    for even in (0, 1):
-        for ns in (even, 1 - even):
-
-            @pl.when(has[ns] & (lax.rem(lat, 2) == even))
-            def _(ns=ns):
-                for copy in row_copies(ns):
-                    copy.start()
+    def send_rows():
+        for even in (0, 1):
+            for ns in (even, 1 - even):
+
+                @pl.when(has[ns] & (lax.rem(lat, 2) == even))
+                def _(ns=ns):
+                    for copy in row_copies(ns):
+                        copy.start()
+
+    @pl.when(lon < n_lon - 1)
+    def _():
+        send_rows()
 
     run(
         read_one,
@@ -510,6 +546,10 @@
         span(first + 1, last - 1),
         slot_one,
     )
+    @pl.when(lon == n_lon - 1)
+    def _():
+        send_rows()
+
     run(
         read_two,
         vtwo,
@@ -526,13 +566,17 @@
         @pl.when(jnp.logical_not(early[d]))
         def _(d=d):
             pl.semaphore_wait(told_sem.at[d], 2 + n_beside)
-            sides[d].start()
+
+        @pl.when(jnp.logical_not(soon[d]))
+        def _(d=d):
+            for copy in sides[d]:
+                copy.start()
             for ns in (0, 1):
                 send_corner(ns, d)
 
     for d in (0, 1):
 
-        @pl.when(jnp.logical_not(early[d]) | (comp == 0))
+        @pl.when(jnp.logical_not(soon[d]) | (comp == 0))
         def _(d=d):
             across[1 + d].start()
 

time: 10.9 us -> 10.8 us (level)
  the two profiles are of different devices: /device:TPU:0 before, /device:TPU:1 now
where the time goes in v4:
time: 10.8 us; the launch traced here: 10.6 us
  Pallas kernels  10.6 us (98%)
    pallas_call x1, Pallas kernels, shards(): pl.pallas_call(functools.partial(exchange, (levels, rows, cols, n_lat, n_...  9.63 us
    pallas_call x1, Pallas kernels, shards(): pl.pallas_call(functools.partial(finish, (levels, rows, cols)), out_shape...  0.95 us

profile of v4, /device:TPU:1, one launch (start us, length us, event | category | flops | bytes accessed | tf_op | source)
XLA Modules:
  0.0 10.6 jit_solution(12432616950488579689)
XLA Ops:
  0.0 9.6 %exchange.1 = (f32[3,16,32,128]{3,2,1,0:T(8,128)S(1)}, f32[3,3,32,128]{3,2,1,0:T(8,128)S(1)}, f32[3,16,128]{2,1,0:T(8,128)S(1)}) custom-call(f32[3,32,16,128]{3,2,1,0:T(8,128)} %bitcast.9, f32[1,32]{1,0:T(1,128)} %push_in.1, f32[1,32]{1,0:T(1,128)} %fill_in.1, f32[32,32]{1,0:T(8,128)} %bitcast.10, s32[16,128]{1,0:T(8,128)} %land_in.1, s32[2,4]{1,0:T(2,128)} %bitcast.11, ...), custom_call_target="tpu_custom_call" | custom-call | tf_op jit(solution)/shard_map/exchange/pallas_call | solution.py:866
  9.6 1.0 %finish.1 = f32[3,32,16,128]{3,2,1,0:T(8,128)} custom-call(f32[3,16,32,128]{3,2,1,0:T(8,128)S(1)} %get-tuple-element.8.main, f32[3,3,32,128]{3,2,1,0:T(8,128)S(1)} %get-tuple-element.9.edge, f32[3,16,128]{2,1,0:T(8,128)S(1)} %get-tuple-element.10.flux), custom_call_target="tpu_custom_call" | custom-call | tf_op jit(solution)/shard_map/finish/pallas_call | solution.py:918

commit v5 on v4

--- a/solution.py
+++ b/solution.py
@@ -812,19 +812,19 @@
     mask_e = jnp.where(j8 == HALO, roll(got_e[:8], -7), roll(ve[:8], -2))
     mask_all = jnp.where(low8, mask_w, mask_e)
     masks = [place(mask_all, own_masks[r], r, 0, False) for r in range(SETS)]
-    for _ in range(2):
-        strips = strip_step(*strips, masks, False)
-    for f in (U, V, PR):
-        for r in range(SETS):
-            change = strips[f][r] - edge[f, r]
-            edge[f, r] = jnp.where(low, roll(change, across_by), change)
-
+    strips = strip_step(*strips, masks, False)
     wait_for(recv_sem.at[5], 9 * rows)
     for f in (U, V, PR):
         value = flux[f]
         for k in range(3):
             value = value + scaled[k] * surf[k, f]
         flux[f] = value
+
+    strips = strip_step(*strips, masks, False)
+    for f in (U, V, PR):
+        for r in range(SETS):
+            change = strips[f][r] - edge[f, r]
+            edge[f, r] = jnp.where(low, roll(change, across_by), change)
 
     wait_for(send_sem.at[0], 2 * side_size + 9 * rows)
     for ns in (0, 1):

time: 10.8 us -> 10.8 us (level)
  the two profiles are of different devices: /device:TPU:1 before, /device:TPU:4 now
where the time goes in v5:
time: 10.8 us; the launch traced here: 10.6 us
  Pallas kernels  10.6 us (98%)
    pallas_call x1, Pallas kernels, shards(): pl.pallas_call(functools.partial(exchange, (levels, rows, cols, n_lat, n_...  9.67 us
    pallas_call x1, Pallas kernels, shards(): pl.pallas_call(functools.partial(finish, (levels, rows, cols)), out_shape...  0.95 us

profile of v5, /device:TPU:4, one launch (start us, length us, event | category | flops | bytes accessed | tf_op | source)
XLA Modules:
  0.0 10.6 jit_solution(14618927971955309290)
XLA Ops:
  0.0 9.7 %exchange.1 = (f32[3,16,32,128]{3,2,1,0:T(8,128)S(1)}, f32[3,3,32,128]{3,2,1,0:T(8,128)S(1)}, f32[3,16,128]{2,1,0:T(8,128)S(1)}) custom-call(f32[3,32,16,128]{3,2,1,0:T(8,128)} %bitcast.9, f32[1,32]{1,0:T(1,128)} %push_in.1, f32[1,32]{1,0:T(1,128)} %fill_in.1, f32[32,32]{1,0:T(8,128)} %bitcast.10, s32[16,128]{1,0:T(8,128)} %land_in.1, s32[2,4]{1,0:T(2,128)} %bitcast.11, ...), custom_call_target="tpu_custom_call" | custom-call | tf_op jit(solution)/shard_map/exchange/pallas_call | solution.py:866
  9.7 1.0 %finish.1 = f32[3,32,16,128]{3,2,1,0:T(8,128)} custom-call(f32[3,16,32,128]{3,2,1,0:T(8,128)S(1)} %get-tuple-element.8.main, f32[3,3,32,128]{3,2,1,0:T(8,128)S(1)} %get-tuple-element.9.edge, f32[3,16,128]{2,1,0:T(8,128)S(1)} %get-tuple-element.10.flux), custom_call_target="tpu_custom_call" | custom-call | tf_op jit(solution)/shard_map/finish/pallas_call | solution.py:918
